TPU v7x, 256 devices: a whole 4x4x8 slice. The times are simulated.
256 devices in a mesh: dist: 2 (over core), rows: 128 (over y, z, x).
Axes of the slice: x: 4, y: 4, z: 8, core: 2. Of those that a mesh axis runs over, the one named last changes fastest.
Arguments:
- holograms: bfloat16 [1, 4, 4, 1024, 1024], P(None, None, 'dist', 'rows'), may hold values from -6 to 6
- propagation: float32 [4], replicated, may hold values from 100 to 1000
- weights: bfloat16 [4, 1024, 1024], P(None, None, 'dist'), may hold values from -0.09375 to 0.09375
- angle_order: int32 [1, 4], replicated, may hold values from 0 to 3, each once within a row
- slab_rows: int32 [128], replicated, may hold values from 0 to 16, as said below
Outputs:
- slab: bfloat16 [2048, 1024], P('rows', 'dist')
Inputs may be any that keep to these rules, and one draw needn't show every extreme that they name: Owners 2j and 2j+1 together own 16 slices: slab_rows[2j] + slab_rows[2j+1] = 16, so owner 2j holds slices 2j 8 onward and owner 2j+1 the rest of that pair's range; in every draw some owner holds 16.
All inputs are finite; a program needn't handle non-finite values.
Results may differ from a plain program's by a relative error of at most 0.02.
Values may be sent and summed in bfloat16 or wider, within the bound.
A program may use at most 128 MiB of HBM per device.

v0:
```python
import math
import jax
import jax.numpy as jnp
from jax import lax
from jax.sharding import PartitionSpec as P

absorb_ratio = 0.1
regularizer = 0.05


def swapped(value, axis, bit):
    mask = 2**bit
    pairs = [(source, source ^ mask) for source in range(lax.axis_size(axis))]
    return lax.ppermute(value, axis, pairs)


def dft_tables(length):
    index = jnp.arange(length, dtype=jnp.int32)
    product = index[:, None] * index[None, :] % length
    turned = product.astype(jnp.float32) * (2.0 * math.pi / length)
    factor = 1.0 / math.sqrt(length)
    return (
        (jnp.cos(turned) * factor).astype(jnp.bfloat16),
        (jnp.sin(turned) * factor).astype(jnp.bfloat16),
    )


def on_device(holograms, propagation, weights, angle_order, slab_rows):
    mbatch, angles, dist_dev, rows_dev, width = holograms.shape
    groups = lax.axis_size("rows")
    capacity = 2 * rows_dev
    cosine, sine = dft_tables(width)
    col_cos = cosine.reshape(groups, rows_dev, width)
    col_sin = sine.reshape(groups, rows_dev, width)
    index = jnp.arange(width, dtype=jnp.int32)
    signed = jnp.where(index < width // 2, index, index - width).astype(jnp.float32)
    device = lax.axis_index("rows")
    local_freq = lax.dynamic_slice_in_dim(signed, device * rows_dev, rows_dev, 0)
    radius = (local_freq[:, None] ** 2 + signed[None, :] ** 2) / float(width * width)
    chirp = propagation[:, None, None] * radius[None]
    transfer = 2.0 * (jnp.sin(chirp) + absorb_ratio * jnp.cos(chirp))
    denom = jnp.sum(transfer * transfer, axis=0) + regularizer
    mine = lax.dynamic_slice_in_dim(transfer, lax.axis_index("dist") * dist_dev, dist_dev, 0)
    parity = device % 2
    offset = parity * slab_rows[device - parity]
    count = slab_rows[device]
    slot = jnp.arange(capacity, dtype=jnp.int32)[:, None]
    source = jnp.arange(capacity, dtype=jnp.int32)[None, :]
    select = ((source == offset + slot) & (slot < count)).astype(jnp.float32)
    flat = holograms[0].reshape(angles * dist_dev * rows_dev, width)
    row_re = jnp.dot(flat, cosine, preferred_element_type=jnp.float32).astype(jnp.bfloat16)
    row_im = (-jnp.dot(flat, sine, preferred_element_type=jnp.float32)).astype(jnp.bfloat16)
    row_re = row_re.reshape(angles * dist_dev, rows_dev, width)
    row_im = row_im.reshape(angles * dist_dev, rows_dev, width)
    pieces = (
        lax.all_to_all(row_re, "rows", split_axis=2, concat_axis=2, tiled=True),
        lax.all_to_all(row_im, "rows", split_axis=2, concat_axis=2, tiled=True),
    )
    items = pieces[0].shape[0]
    real_part = pieces[0].reshape(items, rows_dev, groups, rows_dev)
    imag_part = pieces[1].reshape(items, rows_dev, groups, rows_dev)
    out_re = jnp.einsum("aysk,syq->akq", real_part, col_cos, preferred_element_type=jnp.float32)
    out_re = out_re + jnp.einsum(
        "aysk,syq->akq", imag_part, col_sin, preferred_element_type=jnp.float32
    )
    out_im = jnp.einsum("aysk,syq->akq", imag_part, col_cos, preferred_element_type=jnp.float32)
    out_im = out_im - jnp.einsum(
        "aysk,syq->akq", real_part, col_sin, preferred_element_type=jnp.float32
    )
    spec_re = out_re
    spec_im = out_im
    spec_re = spec_re.reshape(angles, dist_dev, rows_dev, width)
    spec_im = spec_im.reshape(angles, dist_dev, rows_dev, width)
    numer_re = jnp.sum(mine[None] * spec_re, axis=1)
    numer_im = jnp.sum(mine[None] * spec_im, axis=1)
    numer_re, numer_im = (
        lax.psum(numer_re.astype(jnp.bfloat16), "dist").astype(jnp.float32),
        lax.psum(numer_im.astype(jnp.bfloat16), "dist").astype(jnp.float32),
    )
    spec_phase_re = (numer_re / denom).astype(jnp.bfloat16)
    spec_phase_im = (numer_im / denom).astype(jnp.bfloat16)
    half_re = jnp.einsum("akq,qy->aky", spec_phase_re, cosine, preferred_element_type=jnp.float32)
    half_re = (
        half_re - jnp.einsum("akq,qy->aky", spec_phase_im, sine, preferred_element_type=jnp.float32)
    ).astype(jnp.bfloat16)
    half_im = jnp.einsum("akq,qy->aky", spec_phase_im, cosine, preferred_element_type=jnp.float32)
    half_im = (
        half_im + jnp.einsum("akq,qy->aky", spec_phase_re, sine, preferred_element_type=jnp.float32)
    ).astype(jnp.bfloat16)
    pieces = (
        lax.all_to_all(half_re, "rows", split_axis=2, concat_axis=2, tiled=True),
        lax.all_to_all(half_im, "rows", split_axis=2, concat_axis=2, tiled=True),
    )
    items = pieces[0].shape[0]
    real_part = pieces[0].reshape(items, rows_dev, groups, rows_dev)
    imag_part = pieces[1].reshape(items, rows_dev, groups, rows_dev)
    result = jnp.einsum("aksy,skx->ayx", real_part, col_cos, preferred_element_type=jnp.float32)
    phase = (
        result - jnp.einsum("aksy,skx->ayx", imag_part, col_sin, preferred_element_type=jnp.float32)
    ).astype(jnp.bfloat16)
    chosen = weights[0 + angle_order[0]]
    partner = swapped(phase, "rows", 0)
    lower = jnp.where(parity == 1, partner, phase)
    upper = jnp.where(parity == 1, phase, partner)
    paired = jnp.concatenate([lower, upper], axis=1)
    rows_in = jnp.einsum(
        "ij,ajx->aix", select.astype(jnp.bfloat16), paired, preferred_element_type=jnp.float32
    ).astype(jnp.bfloat16)
    recon = jnp.einsum("ayx,axp->yp", rows_in, chosen, preferred_element_type=jnp.float32)
    return recon.astype(jnp.bfloat16)


def solution(mesh):
    return jax.shard_map(
        on_device,
        mesh=mesh,
        in_specs=(P(None, None, "dist", "rows", None), P(), P(None, None, "dist"), P(), P()),
        out_specs=P("rows", "dist"),
        check_vma=False,
    )
```

profile of v0, /device:TPU:2, one launch (start us, length us, event | category | flops | bytes accessed | tf_op | source)
XLA Modules:
  0.0 350.8 jit_solution(18105776519220072496)
XLA Ops:
  7.4 16.1 %fusion.66 = bf16[8,8,1024]{2,1,0:T(8,128)(2,1)S(1)} fusion(bf16[64,1024]{1,0:T(8,128)(2,1)S(1)} %bitcast.132), kind=kOutput, calls=%fused_computation.56 | convolution fusion | flops 151126016 | bytes 262144 | tf_op jit(solution)/shard_map/dot_general | solution.py:52
  28.0 15.8 %all-to-all-start.1 = ((bf16[128,2,256]{2,1,0:T(2,128)(2,1)}), bf16[128,2,256]{2,1,0:T(2,128)(2,1)S(1)}, u32[]{:S(2)}, u32[]{:S(2)}) async-start(bf16[128,2,256]{2,1,0:T(2,128)(2,1)} %reshape.156), calls=%async_computation.1 | async-start | bytes 262144 | tf_op jit(solution)/shard_map/all_to_all | solution.py:57
  43.8 16.0 %fusion.65 = bf16[8,8,1024]{2,1,0:T(8,128)(2,1)S(1)} fusion(bf16[64,1024]{1,0:T(8,128)(2,1)S(1)} %bitcast.133), kind=kOutput, calls=%fused_computation.55 | convolution fusion | flops 151060480 | bytes 262144 | tf_op jit(solution)/shard_map/dot_general | solution.py:51
  65.0 13.8 %all-to-all-start = ((bf16[128,2,256]{2,1,0:T(2,128)(2,1)}), bf16[128,2,256]{2,1,0:T(2,128)(2,1)S(1)}, u32[]{:S(2)}, u32[]{:S(2)}) async-start(bf16[128,2,256]{2,1,0:T(2,128)(2,1)} %reshape.154), calls=%async_computation | async-start | bytes 262144 | tf_op jit(solution)/shard_map/all_to_all | solution.py:56
  78.8 3.5 reshape.157
  82.3 4.3 %copy.30 = bf16[8,8,128,8]{3,2,1,0:T(8,128)(2,1)S(1)} copy(bf16[8,8,128,8]{1,0,3,2:T(8,128)(2,1)} %bitcast.136) | data formatting | bytes 262144 | tf_op jit(solution)/shard_map/reshape | solution.py:61
  86.6 3.6 %all-to-all-done = bf16[128,2,256]{2,1,0:T(2,128)(2,1)S(1)} async-done(((bf16[128,2,256]{2,1,0:T(2,128)(2,1)}), bf16[128,2,256]{2,1,0:T(2,128)(2,1)S(1)}, u32[]{:S(2)}, u32[]{:S(2)}) %all-to-all-start) | async-done | bytes 131104 | tf_op jit(solution)/shard_map/all_to_all | solution.py:56
  90.3 3.5 reshape.155
  93.7 5.4 %copy.28 = bf16[8,8,128,8]{3,2,1,0:T(8,128)(2,1)} copy(bf16[8,8,128,8]{1,0,3,2:T(8,128)(2,1)} %bitcast.137) | data formatting | bytes 262144 | tf_op jit(solution)/shard_map/reshape | solution.py:60
  99.1 16.0 %fusion.39 = f32[8,8,1024]{2,1,0:T(8,128)S(1)} fusion(bf16[8,8,128,8]{3,2,1,0:T(8,128)(2,1)S(1)} %copy.30, s32[128,8]{0,1:T(8,128)S(1)} %multiply_add_fusion), kind=kOutput, calls=%fused_computation.42 | convolution fusion | flops 150994944 | bytes 397312 | tf_op jit(solution)/shard_map/aysk,syq->akq/dot_general | solution.py:66
  115.2 16.1 %fusion.36 = f32[8,8,1024]{2,1,0:T(8,128)S(1)} fusion(bf16[8,8,128,8]{3,2,1,0:T(8,128)(2,1)S(1)} %copy-done.1, s32[128,8]{0,1:T(8,128)S(1)} %multiply_add_fusion), kind=kOutput, calls=%fused_computation.41 | convolution fusion | flops 150994944 | bytes 397312 | tf_op jit(solution)/shard_map/aysk,syq->akq/dot_general | solution.py:62
  131.2 16.5 %fusion.48 = f32[8,8,1024]{2,1,0:T(8,128)S(1)} fusion(f32[8,8,1024]{2,1,0:T(8,128)S(1)} %fusion.39, bf16[8,8,128,8]{3,2,1,0:T(8,128)(2,1)S(1)} %copy-done.1, s32[128,8]{0,1:T(8,128)S(1)} %multiply_add_fusion), kind=kOutput, calls=%fused_computation.45 | convolution fusion | flops 151060480 | bytes 659456 | tf_op jit(solution)/shard_map/aysk,syq->akq/dot_general | solution.py:67
  147.8 16.8 %multiply_reduce_fusion.1 = (bf16[4,8,1024]{2,1,0:T(8,128)(2,1)}, bf16[4,8,1024]{2,1,0:T(8,128)(2,1)}) fusion(f32[2,8,1024]{2,1,0:T(8,128)S(1)} %constant_dynamic-slice_fusion, f32[8,8,1024]{2,1,0:T(8,128)S(1)} %fusion.48, f32[8,8,1024]{2,1,0:T(8,128)S(1)} %fusion.36, bf16[8,8,128,8]{3,2,1,0:T(8,128)(2,1)S(1)} %copy.30, s32[128,8]{0,1:T(8,128)S(1)} %multiply_add_fusion), kind=kOutput, calls=%fused_computation.66 | convolution fusion | flops 151257088 | bytes 856064 | tf_op jit(solution)/shard_map/aysk,syq->akq/dot_general | solution.py:63
  164.6 26.7 %all-reduce.3.cloned.1.call-done = (bf16[4,8,1024]{2,1,0:T(8,128)(2,1)}, bf16[4,8,1024]{2,1,0:T(8,128)(2,1)}) async-done(((bf16[4,8,1024]{2,1,0:T(8,128)(2,1)}, bf16[4,8,1024]{2,1,0:T(8,128)(2,1)}), (bf16[4,8,1024]{2,1,0:T(8,128)(2,1)}, bf16[4,8,1024]{2,1,0:T(8,128)(2,1)})) %all-reduce.3.cloned.1.call-update) | async-done | bytes 131088 | tf_op jit(solution)/shard_map/psum | solution.py:78
  191.3 16.9 %fusion.14 = f32[4,8,1024]{2,1,0:T(8,128)S(1)} fusion(bf16[4,8,1024]{2,1,0:T(8,128)(2,1)} %get-tuple-element.8, f32[8,1024]{1,0:T(8,128)S(1)} %broadcast_add_fusion), kind=kOutput, calls=%fused_computation.25 | convolution fusion | flops 83984384 | bytes 229376 | tf_op jit(solution)/shard_map/akq,qy->aky/dot_general | solution.py:88
  208.2 16.1 %fusion.16 = f32[4,8,1024]{2,1,0:T(8,128)S(1)} fusion(bf16[4,8,1024]{2,1,0:T(8,128)(2,1)S(1)} %copy-done.5, f32[8,1024]{1,0:T(8,128)S(1)} %broadcast_add_fusion), kind=kOutput, calls=%fused_computation.27 | convolution fusion | flops 83984384 | bytes 229376 | tf_op jit(solution)/shard_map/akq,qy->aky/dot_general | solution.py:84
  224.3 15.9 %fusion.79 = bf16[4,8,1024]{2,1,0:T(8,128)(2,1)S(1)} fusion(f32[4,8,1024]{2,1,0:T(8,128)S(1)} %fusion.14, bf16[4,8,1024]{2,1,0:T(8,128)(2,1)S(1)} %copy-done.5, f32[8,1024]{1,0:T(8,128)S(1)} %broadcast_add_fusion), kind=kOutput, calls=%fused_computation.61 | convolution fusion | flops 84049920 | bytes 294912 | tf_op jit(solution)/shard_map/akq,qy->aky/dot_general | solution.py:86
  242.6 14.3 %all-to-all-start.3 = ((bf16[128,2,128]{2,1,0:T(2,128)(2,1)}), bf16[128,2,128]{2,1,0:T(2,128)(2,1)S(1)}, u32[]{:S(2)}, u32[]{:S(2)}) async-start(bf16[128,2,128]{2,1,0:T(2,128)(2,1)} %reshape.160), calls=%async_computation.3 | async-start | bytes 131072 | tf_op jit(solution)/shard_map/all_to_all | solution.py:92
  257.0 15.9 %fusion.82 = bf16[4,8,1024]{2,1,0:T(8,128)(2,1)S(1)} fusion(f32[4,8,1024]{2,1,0:T(8,128)S(1)} %fusion.16, bf16[4,8,1024]{2,1,0:T(8,128)(2,1)S(1)} %copy-done.4, f32[8,1024]{1,0:T(8,128)S(1)} %broadcast_add_fusion), kind=kOutput, calls=%fused_computation.62 | convolution fusion | flops 84049920 | bytes 294912 | tf_op jit(solution)/shard_map/akq,qy->aky/dot_general | solution.py:82
  275.3 13.8 %all-to-all-start.2 = ((bf16[128,2,128]{2,1,0:T(2,128)(2,1)}), bf16[128,2,128]{2,1,0:T(2,128)(2,1)S(1)}, u32[]{:S(2)}, u32[]{:S(2)}) async-start(bf16[128,2,128]{2,1,0:T(2,128)(2,1)} %reshape.158), calls=%async_computation.2 | async-start | bytes 131072 | tf_op jit(solution)/shard_map/all_to_all | solution.py:91
  290.3 5.0 %gather_fusion = bf16[4,1024,512]{2,1,0:T(8,128)(2,1)} fusion(bf16[4,1024,512]{2,1,0:T(8,128)(2,1)} %param.7, s32[1024]{0:T(1024)S(1)} %pad_clamp_fusion), kind=kCustom, calls=%fused_computation | custom fusion | bytes 8388624 | tf_op jit(solution)/shard_map/gather | solution.py:101
  303.7 15.8 %fusion.57 = f32[4,8,1024]{2,1,0:T(8,128)S(1)} fusion(bf16[4,8,128,8]{3,2,1,0:T(8,128)(2,1)S(1)} %copy.36, s32[128,8]{0,1:T(8,128)S(1)} %multiply_add_fusion), kind=kOutput, calls=%fused_computation.51 | convolution fusion | flops 83886080 | bytes 200704 | tf_op jit(solution)/shard_map/aksy,skx->ayx/dot_general | solution.py:97
  319.5 16.0 %fusion.76 = bf16[4,8,1024]{2,1,0:T(8,128)(2,1)S(1)} fusion(f32[4,8,1024]{2,1,0:T(8,128)S(1)} %fusion.57, bf16[4,8,128,8]{3,2,1,0:T(8,128)(2,1)S(1)} %copy.38, s32[128,8]{0,1:T(8,128)S(1)} %multiply_add_fusion), kind=kOutput, calls=%fused_computation.60 | convolution fusion | flops 83951616 | bytes 266240 | tf_op jit(solution)/shard_map/aksy,skx->ayx/dot_general | solution.py:99
  339.9 3.6 %fusion.86 = bf16[16,512]{1,0:T(8,128)(2,1)} fusion(bf16[4,1024,512]{2,1,0:T(8,128)(2,1)} %gather_fusion, bf16[4,8,1024]{2,1,0:T(8,128)(2,1)S(1)} %get-tuple-element.10, bf16[4,8,1024]{2,1,0:T(8,128)(2,1)S(1)} %get-tuple-element.9, s32[16]{0:T(128)S(1)} %iota_add_fusion, pred[16]{0:T(512)(128)(4,1)S(1)} %iota_compare_fusion.1), kind=kOutput, calls=%fused_computation.64 | convolution fusion | flops 69542912 | bytes 4341840 | tf_op jit(solution)/shard_map/ayx,axp->yp/dot_general | solution.py:109
  (47 shorter events, 28.7 us)
Async XLA Ops:
  6.5 0.9 copy-start
  28.0 37.0 %all-to-all-start.1 = ((bf16[128,2,256]{2,1,0:T(2,128)(2,1)}), bf16[128,2,256]{2,1,0:T(2,128)(2,1)S(1)}, u32[]{:S(2)}, u32[]{:S(2)}) async-start(bf16[128,2,256]{2,1,0:T(2,128)(2,1)} %reshape.156), calls=%async_computation.1 | async-start | bytes 262144 | tf_op jit(solution)/shard_map/all_to_all | solution.py:57
  59.7 4.6 %copy-start.3 = (f32[4]{0:T(128)S(1)}, f32[4]{0:T(128)}, u32[]{:S(2)}) copy-start(f32[4]{0:T(128)} %param.6) | copy-start | bytes 52
  65.0 25.3 %all-to-all-start = ((bf16[128,2,256]{2,1,0:T(2,128)(2,1)}), bf16[128,2,256]{2,1,0:T(2,128)(2,1)S(1)}, u32[]{:S(2)}, u32[]{:S(2)}) async-start(bf16[128,2,256]{2,1,0:T(2,128)(2,1)} %reshape.154), calls=%async_computation | async-start | bytes 262144 | tf_op jit(solution)/shard_map/all_to_all | solution.py:56
  78.8 112.5 %all-reduce.3.cloned.1.call-start = ((), (), s32[]{:S(2)}) async-start(), calls=%async_computation.4 | async-start | bytes 262144 | tf_op jit(solution)/shard_map/psum | solution.py:78
  99.1 16.0 %copy-start.1 = (bf16[8,8,128,8]{3,2,1,0:T(8,128)(2,1)S(1)}, bf16[8,8,128,8]{3,2,1,0:T(8,128)(2,1)}, u32[]{:S(2)}) copy-start(bf16[8,8,128,8]{3,2,1,0:T(8,128)(2,1)} %copy.28) | copy-start | bytes 393220
  131.2 33.4 %copy-start.6 = (s32[1,4]{1,0:T(1,128)S(1)}, s32[1,4]{1,0:T(1,128)}, u32[]{:S(2)}) copy-start(s32[1,4]{1,0:T(1,128)} %param.8) | copy-start | bytes 52
  191.3 16.9 %copy-start.5 = (bf16[4,8,1024]{2,1,0:T(8,128)(2,1)S(1)}, bf16[4,8,1024]{2,1,0:T(8,128)(2,1)}, u32[]{:S(2)}) copy-start(bf16[4,8,1024]{2,1,0:T(8,128)(2,1)} %get-tuple-element.7) | copy-start | bytes 196612
  224.3 32.6 %copy-start.4 = (bf16[4,8,1024]{2,1,0:T(8,128)(2,1)S(1)}, bf16[4,8,1024]{2,1,0:T(8,128)(2,1)}, u32[]{:S(2)}) copy-start(bf16[4,8,1024]{2,1,0:T(8,128)(2,1)} %get-tuple-element.8) | copy-start | bytes 196612
  242.6 32.6 %all-to-all-start.3 = ((bf16[128,2,128]{2,1,0:T(2,128)(2,1)}), bf16[128,2,128]{2,1,0:T(2,128)(2,1)S(1)}, u32[]{:S(2)}, u32[]{:S(2)}) async-start(bf16[128,2,128]{2,1,0:T(2,128)(2,1)} %reshape.160), calls=%async_computation.3 | async-start | bytes 131072 | tf_op jit(solution)/shard_map/all_to_all | solution.py:92
  256.9 32.1 %copy-start.2 = (s32[128]{0:T(128)S(1)}, s32[128]{0:T(128)}, u32[]{:S(2)}) copy-start(s32[128]{0:T(128)} %param.9) | copy-start | bytes 1540
  275.3 25.0 %all-to-all-start.2 = ((bf16[128,2,128]{2,1,0:T(2,128)(2,1)}), bf16[128,2,128]{2,1,0:T(2,128)(2,1)S(1)}, u32[]{:S(2)}, u32[]{:S(2)}) async-start(bf16[128,2,128]{2,1,0:T(2,128)(2,1)} %reshape.158), calls=%async_computation.2 | async-start | bytes 131072 | tf_op jit(solution)/shard_map/all_to_all | solution.py:91
  335.6 4.3 %collective-permute-start = (bf16[4,8,1024]{2,1,0:T(8,128)(2,1)S(1)}, bf16[4,8,1024]{2,1,0:T(8,128)(2,1)S(1)}, u32[]{:S(2)}, u32[]{:S(2)}) collective-permute-start(bf16[4,8,1024]{2,1,0:T(8,128)(2,1)S(1)} %fusion.76), channel_id=1, source_target_pairs={{0,1},{1,0},{2,3},{3,2},{4,5},{5,4},{6,7},{7,6},{8,9},{9,8},{10,11... | collective-permute-start | bytes 196616 | tf_op jit(solution)/shard_map/ppermute | solution.py:14
Sparse Core Ops, SparseCore 0:
  164.7 26.5 all-reduce.2
where the time goes:
time: 357 us; the launch traced here: 351 us
  matrix products  198 us (55%)
  starting transfers between devices  59.2 us (17%)
  local copies, waits for them, and re-layouts  43.4 us (12%)
  waiting for transfers between devices  34.3 us (10%)
  between operations  14.7 us (4%)
    psum x1, waiting for transfers between devices, on_device(): lax.psum(numer_im.astype(jnp.bfloat16), 'dist').astype(jnp.float32)  26.7 us
    unnamed x22, local copies, waits for them, and re-layouts  19.5 us
    dot_general x1, matrix products, on_device(): jnp.einsum('akq,qy->aky', spec_phase_re, sine, preferred_element_type=jnp...  16.9 us
    dot_general x1, matrix products, on_device(): jnp.einsum('aysk,syq->akq', imag_part, col_sin, preferred_element_type=jn...  16.8 us
    dot_general x1, matrix products, on_device(): jnp.einsum('aysk,syq->akq', real_part, col_sin, preferred_element_type=jn...  16.5 us
    dot_general x1, matrix products, on_device(): jnp.dot(flat, sine, preferred_element_type=jnp.float32)  16.1 us
    dot_general x1, matrix products, on_device(): jnp.einsum('akq,qy->aky', spec_phase_im, sine, preferred_element_type=jnp...  16.1 us
    dot_general x1, matrix products, on_device(): jnp.einsum('aysk,syq->akq', real_part, col_cos, preferred_element_type=jn...  16.1 us
  transfers between devices with their start and end apart: 6, of which 4 were waited for; matrix products, arithmetic and copies ran while one was open for 16% of the time, Pallas kernels for 0%

commit v1 on v0

--- a/solution.py
+++ b/solution.py
@@ -75,7 +75,7 @@
     numer_im = jnp.sum(mine[None] * spec_im, axis=1)
     numer_re, numer_im = (
         lax.psum(numer_re.astype(jnp.bfloat16), "dist").astype(jnp.float32),
-        lax.psum(numer_im.astype(jnp.bfloat16), "dist").astype(jnp.float32),
+        jnp.sum(lax.all_gather(numer_im.astype(jnp.bfloat16), "dist"), axis=0).astype(jnp.float32),
     )
     spec_phase_re = (numer_re / denom).astype(jnp.bfloat16)
     spec_phase_im = (numer_im / denom).astype(jnp.bfloat16)

time: 357 us -> 342 us (0.958)
  waiting for transfers between devices: 34.3 us -> 16 us
    psum x1, waiting for transfers between devices: 26.7 us -> 8.46 us  [on_device(): lax.psum(numer_re.astype(jnp.bfloat16), 'dist').astype(jnp.float32)]
    unnamed x22 -> x20, local copies, waits for them, and re-layouts: 19.5 us -> 19.5 us
  transfers between devices with their start and end apart: 6 -> 6, of which waited for: 4 -> 4; matrix products, arithmetic and copies ran while one was open for 16% -> 22% of each run, Pallas kernels for 0% -> 0%
where the time goes in v1:
time: 342 us; the launch traced here: 335 us
  matrix products  199 us (58%)
  starting transfers between devices  59.4 us (17%)
  local copies, waits for them, and re-layouts  43.2 us (13%)
  waiting for transfers between devices  16 us (5%)
  between operations  14.7 us (4%)
    unnamed x20, local copies, waits for them, and re-layouts  19.5 us
    dot_general x1, matrix products, on_device(): jnp.einsum('aysk,syq->akq', imag_part, col_sin, preferred_element_type=jn...  17.5 us
    dot_general x1, matrix products, on_device(): jnp.einsum('akq,qy->aky', spec_phase_re, sine, preferred_element_type=jnp...  16.7 us
    dot_general x1, matrix products, on_device(): jnp.einsum('aysk,syq->akq', real_part, col_sin, preferred_element_type=jn...  16.6 us
    dot_general x1, matrix products, on_device(): jnp.einsum('aysk,syq->akq', real_part, col_cos, preferred_element_type=jn...  16.2 us
    dot_general x1, matrix products, on_device(): jnp.einsum('akq,qy->aky', spec_phase_im, cosine, preferred_element_type=j...  16.1 us
    dot_general x1, matrix products, on_device(): jnp.einsum('akq,qy->aky', spec_phase_im, sine, preferred_element_type=jnp...  16.1 us
    dot_general x1, matrix products, on_device(): jnp.dot(flat, sine, preferred_element_type=jnp.float32)  16.1 us
  transfers between devices with their start and end apart: 6, of which 4 were waited for; matrix products, arithmetic and copies ran while one was open for 22% of the time, Pallas kernels for 0%

profile of v1, /device:TPU:2, one launch (start us, length us, event | category | flops | bytes accessed | tf_op | source)
XLA Modules:
  0.0 335.4 jit_solution(17523488243073255542)
XLA Ops:
  7.4 16.1 %fusion.66 = bf16[8,8,1024]{2,1,0:T(8,128)(2,1)S(1)} fusion(bf16[64,1024]{1,0:T(8,128)(2,1)S(1)} %bitcast.133), kind=kOutput, calls=%fused_computation.56 | convolution fusion | flops 151126016 | bytes 262144 | tf_op jit(solution)/shard_map/dot_general | solution.py:52
  28.0 16.0 %all-to-all-start.1 = ((bf16[128,2,256]{2,1,0:T(2,128)(2,1)}), bf16[128,2,256]{2,1,0:T(2,128)(2,1)S(1)}, u32[]{:S(2)}, u32[]{:S(2)}) async-start(bf16[128,2,256]{2,1,0:T(2,128)(2,1)} %reshape.165), calls=%async_computation.1 | async-start | bytes 262144 | tf_op jit(solution)/shard_map/all_to_all | solution.py:57
  44.0 16.0 %fusion.65 = bf16[8,8,1024]{2,1,0:T(8,128)(2,1)S(1)} fusion(bf16[64,1024]{1,0:T(8,128)(2,1)S(1)} %bitcast.134), kind=kOutput, calls=%fused_computation.55 | convolution fusion | flops 151060480 | bytes 262144 | tf_op jit(solution)/shard_map/dot_general | solution.py:51
  65.2 13.8 %all-to-all-start = ((bf16[128,2,256]{2,1,0:T(2,128)(2,1)}), bf16[128,2,256]{2,1,0:T(2,128)(2,1)S(1)}, u32[]{:S(2)}, u32[]{:S(2)}) async-start(bf16[128,2,256]{2,1,0:T(2,128)(2,1)} %reshape.163), calls=%async_computation | async-start | bytes 262144 | tf_op jit(solution)/shard_map/all_to_all | solution.py:56
  79.1 3.5 %reshape.166 = bf16[1024,8,8]{2,1,0:T(8,128)(2,1)} reshape(bf16[128,2,256]{2,1,0:T(2,128)(2,1)S(1)} %all-to-all-done.1) | data formatting | bytes 262144
  82.6 4.3 %copy.30 = bf16[8,8,128,8]{3,2,1,0:T(8,128)(2,1)S(1)} copy(bf16[8,8,128,8]{1,0,3,2:T(8,128)(2,1)} %bitcast.137) | data formatting | bytes 262144 | tf_op jit(solution)/shard_map/reshape | solution.py:61
  86.9 3.6 %all-to-all-done = bf16[128,2,256]{2,1,0:T(2,128)(2,1)S(1)} async-done(((bf16[128,2,256]{2,1,0:T(2,128)(2,1)}), bf16[128,2,256]{2,1,0:T(2,128)(2,1)S(1)}, u32[]{:S(2)}, u32[]{:S(2)}) %all-to-all-start) | async-done | bytes 131104 | tf_op jit(solution)/shard_map/all_to_all | solution.py:56
  90.5 3.5 %reshape.164 = bf16[1024,8,8]{2,1,0:T(8,128)(2,1)} reshape(bf16[128,2,256]{2,1,0:T(2,128)(2,1)S(1)} %all-to-all-done) | data formatting | bytes 262144
  94.0 5.2 %copy.28 = bf16[8,8,128,8]{3,2,1,0:T(8,128)(2,1)} copy(bf16[8,8,128,8]{1,0,3,2:T(8,128)(2,1)} %bitcast.138) | data formatting | bytes 262144 | tf_op jit(solution)/shard_map/reshape | solution.py:60
  99.2 16.0 %fusion.39 = f32[8,8,1024]{2,1,0:T(8,128)S(1)} fusion(bf16[8,8,128,8]{3,2,1,0:T(8,128)(2,1)S(1)} %copy.30, s32[128,8]{0,1:T(8,128)S(1)} %multiply_add_fusion), kind=kOutput, calls=%fused_computation.42 | convolution fusion | flops 150994944 | bytes 397312 | tf_op jit(solution)/shard_map/aysk,syq->akq/dot_general | solution.py:66
  115.2 16.2 %fusion.36 = f32[8,8,1024]{2,1,0:T(8,128)S(1)} fusion(bf16[8,8,128,8]{3,2,1,0:T(8,128)(2,1)S(1)} %copy-done.1, s32[128,8]{0,1:T(8,128)S(1)} %multiply_add_fusion), kind=kOutput, calls=%fused_computation.41 | convolution fusion | flops 150994944 | bytes 397312 | tf_op jit(solution)/shard_map/aysk,syq->akq/dot_general | solution.py:62
  131.5 16.6 %fusion.48 = f32[8,8,1024]{2,1,0:T(8,128)S(1)} fusion(f32[8,8,1024]{2,1,0:T(8,128)S(1)} %fusion.39, bf16[8,8,128,8]{3,2,1,0:T(8,128)(2,1)S(1)} %copy-done.1, s32[128,8]{0,1:T(8,128)S(1)} %multiply_add_fusion), kind=kOutput, calls=%fused_computation.45 | convolution fusion | flops 151060480 | bytes 659456 | tf_op jit(solution)/shard_map/aysk,syq->akq/dot_general | solution.py:67
  148.0 17.5 %multiply_reduce_fusion.1 = (bf16[4,8,1024]{2,1,0:T(8,128)(2,1)}, bf16[4,8,1024]{2,1,0:T(8,128)(2,1)S(1)}) fusion(f32[2,8,1024]{2,1,0:T(8,128)S(1)} %constant_dynamic-slice_fusion, f32[8,8,1024]{2,1,0:T(8,128)S(1)} %fusion.48, f32[8,8,1024]{2,1,0:T(8,128)S(1)} %fusion.36, bf16[8,8,128,8]{3,2,1,0:T(8,128)(2,1)S(1)} %copy.30, s32[128,8]{0,1:T(8,128)S(1)} %multiply_add_fusion), kind=kOutput, calls=%fused_computation.66 | convolution fusion | flops 151257088 | bytes 856064 | tf_op jit(solution)/shard_map/aysk,syq->akq/dot_general | solution.py:63
  167.5 16.1 %fusion.16 = f32[4,8,1024]{2,1,0:T(8,128)S(1)} fusion(bf16[4,8,1024]{2,1,0:T(8,128)(2,1)S(1)} %reduce_sum.42, f32[8,1024]{1,0:T(8,128)S(1)} %broadcast_add_fusion), kind=kOutput, calls=%fused_computation.27 | convolution fusion | flops 83984384 | bytes 229376 | tf_op jit(solution)/shard_map/akq,qy->aky/dot_general | solution.py:84
  183.6 8.5 %all-reduce.2.cloned.1.call-done = bf16[4,8,1024]{2,1,0:T(8,128)(2,1)} async-done(((bf16[4,8,1024]{2,1,0:T(8,128)(2,1)}), bf16[4,8,1024]{2,1,0:T(8,128)(2,1)}) %all-reduce.2.cloned.1.call-update) | async-done | bytes 65552 | tf_op jit(solution)/shard_map/psum | solution.py:77
  192.0 16.7 %fusion.14 = f32[4,8,1024]{2,1,0:T(8,128)S(1)} fusion(bf16[4,8,1024]{2,1,0:T(8,128)(2,1)} %all-reduce.2.cloned.1.call-done, f32[8,1024]{1,0:T(8,128)S(1)} %broadcast_add_fusion), kind=kOutput, calls=%fused_computation.25 | convolution fusion | flops 83984384 | bytes 229376 | tf_op jit(solution)/shard_map/akq,qy->aky/dot_general | solution.py:88
  208.7 16.1 %fusion.79 = bf16[4,8,1024]{2,1,0:T(8,128)(2,1)S(1)} fusion(f32[4,8,1024]{2,1,0:T(8,128)S(1)} %fusion.14, bf16[4,8,1024]{2,1,0:T(8,128)(2,1)S(1)} %reduce_sum.42, f32[8,1024]{1,0:T(8,128)S(1)} %broadcast_add_fusion), kind=kOutput, calls=%fused_computation.61 | convolution fusion | flops 84049920 | bytes 294912 | tf_op jit(solution)/shard_map/akq,qy->aky/dot_general | solution.py:86
  227.2 14.3 %all-to-all-start.3 = ((bf16[128,2,128]{2,1,0:T(2,128)(2,1)}), bf16[128,2,128]{2,1,0:T(2,128)(2,1)S(1)}, u32[]{:S(2)}, u32[]{:S(2)}) async-start(bf16[128,2,128]{2,1,0:T(2,128)(2,1)} %reshape.169), calls=%async_computation.3 | async-start | bytes 131072 | tf_op jit(solution)/shard_map/all_to_all | solution.py:92
  241.5 15.9 %fusion.82 = bf16[4,8,1024]{2,1,0:T(8,128)(2,1)S(1)} fusion(f32[4,8,1024]{2,1,0:T(8,128)S(1)} %fusion.16, bf16[4,8,1024]{2,1,0:T(8,128)(2,1)S(1)} %copy-done.4, f32[8,1024]{1,0:T(8,128)S(1)} %broadcast_add_fusion), kind=kOutput, calls=%fused_computation.62 | convolution fusion | flops 84049920 | bytes 294912 | tf_op jit(solution)/shard_map/akq,qy->aky/dot_general | solution.py:82
  259.8 13.8 %all-to-all-start.2 = ((bf16[128,2,128]{2,1,0:T(2,128)(2,1)}), bf16[128,2,128]{2,1,0:T(2,128)(2,1)S(1)}, u32[]{:S(2)}, u32[]{:S(2)}) async-start(bf16[128,2,128]{2,1,0:T(2,128)(2,1)} %reshape.167), calls=%async_computation.2 | async-start | bytes 131072 | tf_op jit(solution)/shard_map/all_to_all | solution.py:91
  274.8 4.9 %gather_fusion = bf16[4,1024,512]{2,1,0:T(8,128)(2,1)} fusion(bf16[4,1024,512]{2,1,0:T(8,128)(2,1)} %param.7, s32[1024]{0:T(1024)S(1)} %pad_clamp_fusion), kind=kCustom, calls=%fused_computation | custom fusion | bytes 8388624 | tf_op jit(solution)/shard_map/gather | solution.py:101
  288.3 15.8 %fusion.57 = f32[4,8,1024]{2,1,0:T(8,128)S(1)} fusion(bf16[4,8,128,8]{3,2,1,0:T(8,128)(2,1)S(1)} %copy.36, s32[128,8]{0,1:T(8,128)S(1)} %multiply_add_fusion), kind=kOutput, calls=%fused_computation.51 | convolution fusion | flops 83886080 | bytes 200704 | tf_op jit(solution)/shard_map/aksy,skx->ayx/dot_general | solution.py:97
  304.1 16.0 %fusion.76 = bf16[4,8,1024]{2,1,0:T(8,128)(2,1)S(1)} fusion(f32[4,8,1024]{2,1,0:T(8,128)S(1)} %fusion.57, bf16[4,8,128,8]{3,2,1,0:T(8,128)(2,1)S(1)} %copy.38, s32[128,8]{0,1:T(8,128)S(1)} %multiply_add_fusion), kind=kOutput, calls=%fused_computation.60 | convolution fusion | flops 83951616 | bytes 266240 | tf_op jit(solution)/shard_map/aksy,skx->ayx/dot_general | solution.py:99
  324.5 3.6 %fusion.86 = bf16[16,512]{1,0:T(8,128)(2,1)} fusion(bf16[4,1024,512]{2,1,0:T(8,128)(2,1)} %gather_fusion, bf16[4,8,1024]{2,1,0:T(8,128)(2,1)S(1)} %get-tuple-element.8, bf16[4,8,1024]{2,1,0:T(8,128)(2,1)S(1)} %get-tuple-element.7, s32[16]{0:T(128)S(1)} %iota_add_fusion, pred[16]{0:T(512)(128)(4,1)S(1)} %iota_compare_fusion.1), kind=kOutput, calls=%fused_computation.64 | convolution fusion | flops 69542912 | bytes 4341840 | tf_op jit(solution)/shard_map/ayx,axp->yp/dot_general | solution.py:109
  (47 shorter events, 30.6 us)
Async XLA Ops:
  6.5 0.9 copy-start
  28.0 37.2 %all-to-all-start.1 = ((bf16[128,2,256]{2,1,0:T(2,128)(2,1)}), bf16[128,2,256]{2,1,0:T(2,128)(2,1)S(1)}, u32[]{:S(2)}, u32[]{:S(2)}) async-start(bf16[128,2,256]{2,1,0:T(2,128)(2,1)} %reshape.165), calls=%async_computation.1 | async-start | bytes 262144 | tf_op jit(solution)/shard_map/all_to_all | solution.py:57
  44.0 16.2 %copy-start.3 = (f32[4]{0:T(128)S(1)}, f32[4]{0:T(128)}, u32[]{:S(2)}) copy-start(f32[4]{0:T(128)} %param.6) | copy-start | bytes 52
  60.0 5.2 %copy-start.5 = (s32[1,4]{1,0:T(1,128)S(1)}, s32[1,4]{1,0:T(1,128)}, u32[]{:S(2)}) copy-start(s32[1,4]{1,0:T(1,128)} %param.8) | copy-start | bytes 52
  65.2 25.3 %all-to-all-start = ((bf16[128,2,256]{2,1,0:T(2,128)(2,1)}), bf16[128,2,256]{2,1,0:T(2,128)(2,1)S(1)}, u32[]{:S(2)}, u32[]{:S(2)}) async-start(bf16[128,2,256]{2,1,0:T(2,128)(2,1)} %reshape.163), calls=%async_computation | async-start | bytes 262144 | tf_op jit(solution)/shard_map/all_to_all | solution.py:56
  79.0 113.0 %all-reduce.2.cloned.1.call-start = ((), (), s32[]{:S(2)}) async-start(), calls=%async_computation.4 | async-start | bytes 131072 | tf_op jit(solution)/shard_map/psum | solution.py:77
  99.2 16.1 %copy-start.1 = (bf16[8,8,128,8]{3,2,1,0:T(8,128)(2,1)S(1)}, bf16[8,8,128,8]{3,2,1,0:T(8,128)(2,1)}, u32[]{:S(2)}) copy-start(bf16[8,8,128,8]{3,2,1,0:T(8,128)(2,1)} %copy.28) | copy-start | bytes 393220
  208.7 32.8 %copy-start.4 = (bf16[4,8,1024]{2,1,0:T(8,128)(2,1)S(1)}, bf16[4,8,1024]{2,1,0:T(8,128)(2,1)}, u32[]{:S(2)}) copy-start(bf16[4,8,1024]{2,1,0:T(8,128)(2,1)} %all-reduce.2.cloned.1.call-done) | copy-start | bytes 196612
  227.2 32.6 %all-to-all-start.3 = ((bf16[128,2,128]{2,1,0:T(2,128)(2,1)}), bf16[128,2,128]{2,1,0:T(2,128)(2,1)S(1)}, u32[]{:S(2)}, u32[]{:S(2)}) async-start(bf16[128,2,128]{2,1,0:T(2,128)(2,1)} %reshape.169), calls=%async_computation.3 | async-start | bytes 131072 | tf_op jit(solution)/shard_map/all_to_all | solution.py:92
  241.5 32.2 %copy-start.2 = (s32[128]{0:T(128)S(1)}, s32[128]{0:T(128)}, u32[]{:S(2)}) copy-start(s32[128]{0:T(128)} %param.9) | copy-start | bytes 1540
  259.8 25.0 %all-to-all-start.2 = ((bf16[128,2,128]{2,1,0:T(2,128)(2,1)}), bf16[128,2,128]{2,1,0:T(2,128)(2,1)S(1)}, u32[]{:S(2)}, u32[]{:S(2)}) async-start(bf16[128,2,128]{2,1,0:T(2,128)(2,1)} %reshape.167), calls=%async_computation.2 | async-start | bytes 131072 | tf_op jit(solution)/shard_map/all_to_all | solution.py:91
  320.1 4.3 %collective-permute-start = (bf16[4,8,1024]{2,1,0:T(8,128)(2,1)S(1)}, bf16[4,8,1024]{2,1,0:T(8,128)(2,1)S(1)}, u32[]{:S(2)}, u32[]{:S(2)}) collective-permute-start(bf16[4,8,1024]{2,1,0:T(8,128)(2,1)S(1)} %fusion.76), channel_id=1, source_target_pairs={{0,1},{1,0},{2,3},{3,2},{4,5},{5,4},{6,7},{7,6},{8,9},{9,8},{10,11... | collective-permute-start | bytes 196616 | tf_op jit(solution)/shard_map/ppermute | solution.py:14
Sparse Core Ops, SparseCore 0:
  165.7 26.3 all-reduce.1
